TPU v7x, 32 devices: a whole 2x2x4 slice. The times are simulated.
32 devices in a mesh: parts: 2 (over x), rows: 16 (over z, y, core).
Axes of the slice: x: 2, y: 2, z: 4, core: 2. Of those that a mesh axis runs over, the one named last changes fastest.
Arguments:
- rhs: float32 [3, 12288, 256], P(None, 'rows', 'parts'), parts along dimension 2, may hold values from -6 to 6
- diag_inv: float32 [3, 12288, 768], P(None, 'rows'), may hold values from -0.21875 to 0.21875
- tiles: float32 [2, 32, 768, 768], P(None, 'rows'), may hold values from -0.15625 to 0.15625
- dest: int32 [2, 16, 2], P(None, 'rows'), may hold values from 0 to 15, all different within a row; in each aligned block of 16 rows (0 to 15, 16 to 31, ..., all dimensions but the last counted through in order) at most 4 rows name the same one
- obs_weight: float32 [12288], P('rows'), may hold values from -0.108253175 to 0.108253175, as said below
Outputs:
- solution: float32 [3, 12288, 256], P(None, 'rows', 'parts'), parts along dimension 2
- observed: float32 [256], P('parts'), parts along dimension 0
There are 2 independent parts, one for each index of `parts`. A program takes and returns all parts, laid end to end along the dimension named above; an argument that names none is the same for every part. Nothing has to cross between parts.
Inputs may be any that keep to these rules, and one draw needn't show every extreme that they name: `dest`: in each of the two levels, the two entries of a supernode differ, and no supernode of the next level is named more than 4 times. `obs_weight`: finite weights.
All inputs are finite; a program needn't handle non-finite values.
Results may differ from a plain program's by a relative error of at most 0.00029.
Values sent between devices are 32-bit elements; how exact they have to be, the bound alone decides.
No kernel may reach another device: no remote copies, remote signals or barrier semaphores. Data moves between devices by JAX's collectives and lax.ppermute only.
A program may use at most 128 MiB of HBM per device.

v0:
```python
import jax
import jax.numpy as jnp
from jax import lax
from jax.sharding import PartitionSpec as P


def collect_updates(solved_block, tiles_level, pattern_level):
    products = jnp.einsum(
        "kab,bc->kac",
        tiles_level,
        solved_block,
        precision=lax.Precision.HIGHEST,
        preferred_element_type=jnp.float32,
    )
    block_rows = solved_block.shape[0]
    width = products.shape[2]
    count = lax.axis_size("rows")
    sliced = lax.all_to_all(products, "rows", split_axis=1, concat_axis=0, tiled=True)
    owners = jnp.arange(count, dtype=jnp.int32)
    flat_targets = pattern_level.reshape(-1)
    matches = (owners[:, None] == flat_targets[None, :]).astype(jnp.float32)
    partial_value = jnp.einsum("mq,qac->mac", matches, sliced, precision=lax.Precision.HIGHEST)
    returned = lax.all_to_all(partial_value, "rows", split_axis=0, concat_axis=0, tiled=True)
    return returned.reshape(block_rows, width)


def body(rhs, diag_inv, tiles, dest, obs_weight):
    pattern = lax.all_gather(dest, "rows", axis=1, tiled=True)
    current = rhs[0]
    solved_levels = []
    solved_block = current
    for section in range(3):
        solved_block = jnp.dot(
            diag_inv[section],
            current,
            precision=lax.Precision.HIGHEST,
            preferred_element_type=jnp.float32,
        )
        solved_levels.append(solved_block)
        if section < 2:
            current = rhs[section + 1] - collect_updates(
                solved_block, tiles[section], pattern[section]
            )
    partial_sum = jnp.dot(
        obs_weight,
        solved_block,
        precision=lax.Precision.HIGHEST,
        preferred_element_type=jnp.float32,
    )
    observed = lax.psum(partial_sum, "rows")
    return (jnp.stack(solved_levels), observed)


def solution(mesh):
    in_specs = (
        P(None, "rows", "parts"),
        P(None, "rows", None),
        P(None, "rows", None, None),
        P(None, "rows", None),
        P("rows"),
    )
    out_specs = (P(None, "rows", "parts"), P("parts"))
    return jax.shard_map(body, mesh=mesh, in_specs=in_specs, out_specs=out_specs, check_vma=False)
```

profile of v0, /device:TPU:0, one launch (start us, length us, event | category | flops | bytes accessed | tf_op | source)
XLA Modules:
  0.0 156.5 jit_solution(14306570408259959369)
XLA Ops:
  0.6 3.7 %fusion.10 = f32[768,128]{1,0:T(8,128)S(1)} fusion(f32[3,768,768]{2,1,0:T(8,128)} %param.6, f32[3,768,128]{2,1,0:T(8,128)} %param.5), kind=kOutput, calls=%fused_computation.10 | convolution fusion | flops 905969664 | bytes 3145728 | tf_op jit(solution)/shard_map/dot_general | solution.py:33
  4.3 7.4 %fusion.15 = f32[2,768,128]{1,2,0:T(8,128)S(1)} fusion(f32[2,2,768,768]{3,2,1,0:T(8,128)} %param.7, f32[768,128]{1,0:T(8,128)S(1)} %fusion.10), kind=kOutput, calls=%fused_computation.15 | convolution fusion | flops 1811939328 | bytes 5898240 | tf_op jit(solution)/shard_map/kab,bc->kac/dot_general | solution.py:8
  11.7 1.2 copy.23
  12.9 7.5 %all-to-all-start = ((f32[2,768,128]{2,0,1:T(2,128)}), f32[2,768,128]{2,0,1:T(2,128)S(1)}, u32[]{:S(2)}, u32[]{:S(2)}) async-start(f32[2,768,128]{2,0,1:T(2,128)} %copy.23), calls=%async_computation | async-start | bytes 1572864 | tf_op jit(solution)/shard_map/all_to_all | solution.py:18
  20.4 29.2 %all_gather.3 = s32[2,16,2]{2,0,1:T(2,128)S(1)} all-gather(s32[2,1,2]{2,0,1:T(2,128)S(1)} %bitcast.82), channel_id=1, replica_groups=mesh['parts'=2,'rows'=16] {'rows'}, dimensions={1}, use_global_device_ids=true | all-gather | bytes 272 | tf_op jit(solution)/shard_map/all_gather | solution.py:28
  49.8 0.6 copy.25
  50.5 0.4 fusion.29
  50.8 0.1 copy.26
  51.0 16.7 %all_to_all.46 = f32[16,48,128]{2,1,0:T(8,128)S(1)} all-to-all(f32[16,48,128]{2,1,0:T(8,128)S(1)} %copy.26), channel_id=1, replica_groups=mesh['parts'=2,'rows'=16] {'rows'}, dimensions={0} | all-to-all | bytes 786432 | tf_op jit(solution)/shard_map/all_to_all | solution.py:23
  67.8 3.8 %fusion.8 = f32[128,768]{1,0:T(8,128)S(1)} fusion(f32[3,768,768]{2,1,0:T(8,128)} %param.6, f32[1,768,128]{2,1,0:T(8,128)S(1)} %bitcast_subtract_fusion.1), kind=kOutput, calls=%fused_computation.8 | convolution fusion | flops 905969664 | bytes 3145728 | tf_op jit(solution)/shard_map/dot_general | solution.py:33
  71.5 5.0 %fusion.18 = f32[2,768,128]{1,2,0:T(8,128)S(1)} fusion(f32[2,2,768,768]{3,2,1,0:T(8,128)S(1)} %copy-done, f32[128,768]{1,0:T(8,128)S(1)} %fusion.8), kind=kOutput, calls=%fused_computation.16 | convolution fusion | flops 1811939328 | bytes 5898240 | tf_op jit(solution)/shard_map/kab,bc->kac/dot_general | solution.py:8
  76.5 1.2 copy.28
  77.7 3.6 %all-to-all-start.2 = ((f32[2,768,128]{2,0,1:T(2,128)}), f32[2,768,128]{2,0,1:T(2,128)S(1)}, u32[]{:S(2)}, u32[]{:S(2)}) async-start(f32[2,768,128]{2,0,1:T(2,128)} %copy.28), calls=%async_computation.2 | async-start | bytes 1572864 | tf_op jit(solution)/shard_map/all_to_all | solution.py:18
  81.4 18.6 %all-to-all-done.2 = f32[2,768,128]{2,0,1:T(2,128)S(1)} async-done(((f32[2,768,128]{2,0,1:T(2,128)}), f32[2,768,128]{2,0,1:T(2,128)S(1)}, u32[]{:S(2)}, u32[]{:S(2)}) %all-to-all-start.2) | async-done | bytes 786464 | tf_op jit(solution)/shard_map/all_to_all | solution.py:18
  100.0 0.6 copy.30
  100.6 0.4 fusion.32
  101.0 0.9 copy.31
  101.9 5.3 %all-to-all-start.3 = ((f32[16,48,128]{2,1,0:T(8,128)}), f32[16,48,128]{2,1,0:T(8,128)S(1)}, u32[]{:S(2)}, u32[]{:S(2)}) async-start(f32[16,48,128]{2,1,0:T(8,128)} %copy.31), calls=%async_computation.3 | async-start | bytes 786432 | tf_op jit(solution)/shard_map/all_to_all | solution.py:23
  107.3 0.2 copy.27
  107.4 12.0 %all-to-all-done.3 = f32[16,48,128]{2,1,0:T(8,128)S(1)} async-done(((f32[16,48,128]{2,1,0:T(8,128)}), f32[16,48,128]{2,1,0:T(8,128)S(1)}, u32[]{:S(2)}, u32[]{:S(2)}) %all-to-all-start.3) | async-done | bytes 393248 | tf_op jit(solution)/shard_map/all_to_all | solution.py:23
  119.4 3.7 %fusion.6 = f32[128,768]{0,1:T(8,128)S(1)} fusion(f32[3,768,768]{2,1,0:T(8,128)} %param.6, f32[1,768,128]{2,1,0:T(8,128)S(1)} %bitcast_subtract_fusion), kind=kOutput, calls=%fused_computation.6 | convolution fusion | flops 905969664 | bytes 3145728 | tf_op jit(solution)/shard_map/dot_general | solution.py:33
  123.1 0.3 convolution_bitcast_fusion
  123.4 32.0 %psum.7 = f32[128]{0:T(128)} all-reduce(f32[128]{0:T(128)S(1)} %convolution_bitcast_fusion), channel_id=1, replica_groups=mesh['parts'=2,'rows'=16] {'rows'}, use_global_device_ids=true, to_apply=%region_0.0 | all-reduce | flops 128 | bytes 1024 | tf_op jit(solution)/shard_map/psum | solution.py:50
  155.4 1.1 pad_maximum_fusion
  (17 shorter events, 0.4 us)
Async XLA Ops:
  11.7 8.7 %copy-start.3 = (s32[2,1,2]{2,1,0:T(1,128)S(1)}, s32[2,1,2]{2,1,0:T(1,128)}, u32[]{:S(2)}) copy-start(s32[2,1,2]{2,1,0:T(1,128)} %param.8) | copy-start | bytes 52
  12.9 54.8 %copy-start.1 = (f32[3,768,128]{2,1,0:T(8,128)S(1)}, f32[3,768,128]{2,1,0:T(8,128)}, u32[]{:S(2)}) copy-start(f32[3,768,128]{2,1,0:T(8,128)} %param.5) | copy-start | bytes 3538948
  12.9 36.9 %all-to-all-start = ((f32[2,768,128]{2,0,1:T(2,128)}), f32[2,768,128]{2,0,1:T(2,128)S(1)}, u32[]{:S(2)}, u32[]{:S(2)}) async-start(f32[2,768,128]{2,0,1:T(2,128)} %copy.23), calls=%async_computation | async-start | bytes 1572864 | tf_op jit(solution)/shard_map/all_to_all | solution.py:18
  49.8 21.8 %copy-start = (f32[2,2,768,768]{3,2,1,0:T(8,128)S(1)}, f32[2,2,768,768]{3,2,1,0:T(8,128)}, u32[]{:S(2)}) copy-start(f32[2,2,768,768]{3,2,1,0:T(8,128)} %param.7) | copy-start | bytes 28311556
  77.7 22.3 %all-to-all-start.2 = ((f32[2,768,128]{2,0,1:T(2,128)}), f32[2,768,128]{2,0,1:T(2,128)S(1)}, u32[]{:S(2)}, u32[]{:S(2)}) async-start(f32[2,768,128]{2,0,1:T(2,128)} %copy.28), calls=%async_computation.2 | async-start | bytes 1572864 | tf_op jit(solution)/shard_map/all_to_all | solution.py:18
  100.0 7.2 %copy-start.2 = (f32[768]{0:T(1024)S(1)}, f32[768]{0:T(1024)}, u32[]{:S(2)}) copy-start(f32[768]{0:T(1024)} %param.9) | copy-start | bytes 9220
  101.9 17.5 %all-to-all-start.3 = ((f32[16,48,128]{2,1,0:T(8,128)}), f32[16,48,128]{2,1,0:T(8,128)S(1)}, u32[]{:S(2)}, u32[]{:S(2)}) async-start(f32[16,48,128]{2,1,0:T(8,128)} %copy.31), calls=%async_computation.3 | async-start | bytes 786432 | tf_op jit(solution)/shard_map/all_to_all | solution.py:23
where the time goes:
time: 157 us
  blocking collectives  77.9 us (50%)
  waiting for transfers between devices  30.5 us (19%)
  matrix products  24.5 us (16%)
  starting transfers between devices  16.5 us (11%)
  local copies, waits for them, and re-layouts  5.05 us (3%)
    psum x1, blocking collectives, body(): observed = lax.psum(partial_sum, 'rows')  32 us
    all_gather x1, blocking collectives, body(): pattern = lax.all_gather(dest, 'rows', axis=1, tiled=True)  29.2 us
    all_to_all x2, waiting for transfers between devices, collect_updates(): lax.all_to_all(products, 'rows', split_axis=1, concat_axis=0, tiled=True)  18.6 us
    all_to_all x1, blocking collectives, collect_updates(): lax.all_to_all(partial_value, 'rows', split_axis=0, concat_axis=0, tiled=...  16.7 us
    dot_general x2, matrix products, collect_updates(): jnp.einsum('kab,bc->kac', tiles_level, solved_block, precision=lax.Precis...  12.3 us
    all_to_all x1, waiting for transfers between devices, collect_updates(): lax.all_to_all(partial_value, 'rows', split_axis=0, concat_axis=0, tiled=...  12 us
    all_to_all x2, starting transfers between devices, collect_updates(): lax.all_to_all(products, 'rows', split_axis=1, concat_axis=0, tiled=True)  11.2 us
    dot_general x3, matrix products, body(): jnp.dot(diag_inv[section], current, precision=lax.Precision.HIGHEST, pref...  11.1 us
  transfers between devices with their start and end apart: 3, of which 2 were waited for; matrix products, arithmetic and copies ran while one was open for 0% of the time, Pallas kernels for 0%

commit v1 on v0

--- a/solution.py
+++ b/solution.py
@@ -15,7 +15,10 @@
     block_rows = solved_block.shape[0]
     width = products.shape[2]
     count = lax.axis_size("rows")
-    sliced = lax.all_to_all(products, "rows", split_axis=1, concat_axis=0, tiled=True)
+    sliced = jnp.concatenate(
+        lax.all_to_all(jnp.stack(jnp.split(products, lax.axis_size("rows"), axis=1)), "rows", 0, 0),
+        axis=0,
+    )
     owners = jnp.arange(count, dtype=jnp.int32)
     flat_targets = pattern_level.reshape(-1)
     matches = (owners[:, None] == flat_targets[None, :]).astype(jnp.float32)

time: 157 us -> 190 us (1.21)
  local copies, waits for them, and re-layouts: 5.05 us -> 36.3 us
  matrix products: 24.5 us -> 26.7 us
    unnamed x9 -> x53, local copies, waits for them, and re-layouts: 0.03 us -> 19.6 us
    another operation x0 -> x36, local copies, waits for them, and re-layouts: none -> 14 us  [collect_updates(): jnp.stack(jnp.split(products, lax.axis_size('rows'), axis=1))]
    dot_general x2 -> x0, local copies, waits for them, and re-layouts: 2.33 us -> none  [collect_updates(): jnp.einsum('kab,bc->kac', tiles_level, solved_block, precision=lax.Precis...]
    dot_general x2, matrix products: 12.3 us -> 14.5 us  [collect_updates(): jnp.einsum('kab,bc->kac', tiles_level, solved_block, precision=lax.Precis...]
  transfers between devices with their start and end apart: 3 -> 3, of which waited for: 2 -> 2; matrix products, arithmetic and copies ran while one was open for 0% -> 1% of each run, Pallas kernels for 0% -> 0%
where the time goes in v1:
time: 190 us
  blocking collectives  77.6 us (41%)
  local copies, waits for them, and re-layouts  36.3 us (19%)
  waiting for transfers between devices  30.5 us (16%)
  matrix products  26.7 us (14%)
  starting transfers between devices  16.4 us (9%)
    psum x1, blocking collectives, body(): observed = lax.psum(partial_sum, 'rows')  32 us
    all_gather x1, blocking collectives, body(): pattern = lax.all_gather(dest, 'rows', axis=1, tiled=True)  29.2 us
    unnamed x53, local copies, waits for them, and re-layouts  19.6 us
    all_to_all x2, waiting for transfers between devices, collect_updates(): lax.all_to_all(jnp.stack(jnp.split(products, lax.axis_size('rows'), axis=...  18.5 us
    all_to_all x1, blocking collectives, collect_updates(): lax.all_to_all(partial_value, 'rows', split_axis=0, concat_axis=0, tiled=...  16.4 us
    dot_general x2, matrix products, collect_updates(): jnp.einsum('kab,bc->kac', tiles_level, solved_block, precision=lax.Precis...  14.5 us
    another operation x36, local copies, waits for them, and re-layouts, collect_updates(): jnp.stack(jnp.split(products, lax.axis_size('rows'), axis=1))  14 us
    all_to_all x1, waiting for transfers between devices, collect_updates(): lax.all_to_all(partial_value, 'rows', split_axis=0, concat_axis=0, tiled=...  12 us
  transfers between devices with their start and end apart: 3, of which 2 were waited for; matrix products, arithmetic and copies ran while one was open for 1% of the time, Pallas kernels for 0%

profile of v1, /device:TPU:0, one launch (start us, length us, event | category | flops | bytes accessed | tf_op | source)
XLA Modules:
  0.0 189.7 jit_solution(6801633247055015809)
XLA Ops:
  0.6 3.7 %fusion.10 = f32[768,128]{1,0:T(8,128)S(1)} fusion(f32[3,768,768]{2,1,0:T(8,128)} %param.6, f32[3,768,128]{2,1,0:T(8,128)} %param.5), kind=kOutput, calls=%fused_computation.10 | convolution fusion | flops 905969664 | bytes 3145728 | tf_op jit(solution)/shard_map/dot_general | solution.py:36
  4.3 7.4 %fusion.15 = f32[2,768,128]{1,2,0:T(8,128)S(1)} fusion(f32[2,2,768,768]{3,2,1,0:T(8,128)} %param.7, f32[768,128]{1,0:T(8,128)S(1)} %fusion.10), kind=kOutput, calls=%fused_computation.15 | convolution fusion | flops 1811939328 | bytes 5898240 | tf_op jit(solution)/shard_map/kab,bc->kac/dot_general | solution.py:8
  23.5 7.4 %all-to-all-start = ((f32[16,2,48,128]{3,2,1,0:T(8,128)}), f32[16,2,48,128]{3,2,1,0:T(8,128)S(1)}, u32[]{:S(2)}, u32[]{:S(2)}) async-start(f32[16,2,48,128]{3,2,1,0:T(8,128)} %constant_dynamic-update-slice_fusion), calls=%async_computation | async-start | bytes 1572864 | tf_op jit(solution)/shard_map/all_to_all | solution.py:19
  31.0 29.2 %all_gather.3 = s32[2,16,2]{2,0,1:T(2,128)S(1)} all-gather(s32[2,1,2]{2,0,1:T(2,128)S(1)} %bitcast.138), channel_id=1, replica_groups=mesh['parts'=2,'rows'=16] {'rows'}, dimensions={1}, use_global_device_ids=true | all-gather | bytes 272 | tf_op jit(solution)/shard_map/all_gather | solution.py:31
  61.8 16.4 %all_to_all.20 = f32[16,48,128]{2,1,0:T(8,128)S(1)} all-to-all(f32[16,48,128]{2,1,0:T(8,128)S(1)} %copy.38), channel_id=1, replica_groups=mesh['parts'=2,'rows'=16] {'rows'}, dimensions={0} | all-to-all | bytes 786432 | tf_op jit(solution)/shard_map/all_to_all | solution.py:26
  78.3 3.8 %fusion.8 = f32[128,768]{1,0:T(8,128)S(1)} fusion(f32[3,768,768]{2,1,0:T(8,128)} %param.6, f32[1,768,128]{2,1,0:T(8,128)S(1)} %bitcast_subtract_fusion.1), kind=kOutput, calls=%fused_computation.8 | convolution fusion | flops 905969664 | bytes 3145728 | tf_op jit(solution)/shard_map/dot_general | solution.py:36
  82.1 7.2 %fusion.18 = f32[2,768,128]{1,2,0:T(8,128)S(1)} fusion(f32[2,2,768,768]{3,2,1,0:T(8,128)} %param.7, f32[128,768]{1,0:T(8,128)S(1)} %fusion.8), kind=kOutput, calls=%fused_computation.16 | convolution fusion | flops 1811939328 | bytes 5898240 | tf_op jit(solution)/shard_map/kab,bc->kac/dot_general | solution.py:8
  89.3 1.3 slice_bitcast_fusion
  90.5 1.6 copy.55
  92.1 1.6 copy.54
  93.7 1.6 copy.53
  95.3 1.6 copy.52
  96.9 0.7 copy.51
  97.6 0.7 copy.50
  98.3 0.7 copy.49
  105.3 1.4 constant_dynamic-update-slice_fusion.23
  111.1 3.6 %all-to-all-start.2 = ((f32[16,2,48,128]{3,2,1,0:T(8,128)}), f32[16,2,48,128]{3,2,1,0:T(8,128)S(1)}, u32[]{:S(2)}, u32[]{:S(2)}) async-start(f32[16,2,48,128]{3,2,1,0:T(8,128)} %constant_dynamic-update-slice_fusion.16), calls=%async_computation.2 | async-start | bytes 1572864 | tf_op jit(solution)/shard_map/all_to_all | solution.py:19
  114.9 18.5 %all-to-all-done.2 = f32[16,2,48,128]{3,2,1,0:T(8,128)S(1)} async-done(((f32[16,2,48,128]{3,2,1,0:T(8,128)}), f32[16,2,48,128]{3,2,1,0:T(8,128)S(1)}, u32[]{:S(2)}, u32[]{:S(2)}) %all-to-all-start.2) | async-done | bytes 786464 | tf_op jit(solution)/shard_map/all_to_all | solution.py:19
  134.2 0.9 copy.57
  135.1 5.3 %all-to-all-start.3 = ((f32[16,48,128]{2,1,0:T(8,128)}), f32[16,48,128]{2,1,0:T(8,128)S(1)}, u32[]{:S(2)}, u32[]{:S(2)}) async-start(f32[16,48,128]{2,1,0:T(8,128)} %copy.57), calls=%async_computation.3 | async-start | bytes 786432 | tf_op jit(solution)/shard_map/all_to_all | solution.py:26
  140.6 12.0 %all-to-all-done.3 = f32[16,48,128]{2,1,0:T(8,128)S(1)} async-done(((f32[16,48,128]{2,1,0:T(8,128)}), f32[16,48,128]{2,1,0:T(8,128)S(1)}, u32[]{:S(2)}, u32[]{:S(2)}) %all-to-all-start.3) | async-done | bytes 393248 | tf_op jit(solution)/shard_map/all_to_all | solution.py:26
  152.6 3.7 %fusion.6 = f32[128,768]{0,1:T(8,128)S(1)} fusion(f32[3,768,768]{2,1,0:T(8,128)} %param.6, f32[1,768,128]{2,1,0:T(8,128)S(1)} %bitcast_subtract_fusion), kind=kOutput, calls=%fused_computation.6 | convolution fusion | flops 905969664 | bytes 3145728 | tf_op jit(solution)/shard_map/dot_general | solution.py:36
  156.6 32.0 %psum.7 = f32[128]{0:T(128)} all-reduce(f32[128]{0:T(128)S(1)} %convolution_bitcast_fusion), channel_id=1, replica_groups=mesh['parts'=2,'rows'=16] {'rows'}, use_global_device_ids=true, to_apply=%region_0.0 | all-reduce | flops 128 | bytes 1024 | tf_op jit(solution)/shard_map/psum | solution.py:53
  188.6 1.1 pad_maximum_fusion
  (93 shorter events, 25.4 us)
Async XLA Ops:
  12.8 18.2 %copy-start.10 = (s32[2,1,2]{2,1,0:T(1,128)S(1)}, s32[2,1,2]{2,1,0:T(1,128)}, u32[]{:S(2)}) copy-start(s32[2,1,2]{2,1,0:T(1,128)} %param.8) | copy-start | bytes 52
  23.5 37.3 %all-to-all-start = ((f32[16,2,48,128]{3,2,1,0:T(8,128)}), f32[16,2,48,128]{3,2,1,0:T(8,128)S(1)}, u32[]{:S(2)}, u32[]{:S(2)}) async-start(f32[16,2,48,128]{3,2,1,0:T(8,128)} %constant_dynamic-update-slice_fusion), calls=%async_computation | async-start | bytes 1572864 | tf_op jit(solution)/shard_map/all_to_all | solution.py:19
  30.9 47.3 %copy-start = (f32[3,768,128]{2,1,0:T(8,128)S(1)}, f32[3,768,128]{2,1,0:T(8,128)}, u32[]{:S(2)}) copy-start(f32[3,768,128]{2,1,0:T(8,128)} %param.5) | copy-start | bytes 3538948
  97.6 11.7 %copy-start.3 = (f32[1,2,48,128]{3,2,1,0:T(8,128)S(1)}, f32[1,2,48,128]{3,2,1,0:T(8,128)}, u32[]{:S(2)}) copy-start(f32[1,2,48,128]{3,2,1,0:T(8,128)} %copy.53) | copy-start | bytes 147460
  97.6 12.3 %copy-start.2 = (f32[1,2,48,128]{3,2,1,0:T(8,128)S(1)}, f32[1,2,48,128]{3,2,1,0:T(8,128)}, u32[]{:S(2)}) copy-start(f32[1,2,48,128]{3,2,1,0:T(8,128)} %copy.54) | copy-start | bytes 147460
  97.6 12.9 %copy-start.1 = (f32[1,2,48,128]{3,2,1,0:T(8,128)S(1)}, f32[1,2,48,128]{3,2,1,0:T(8,128)}, u32[]{:S(2)}) copy-start(f32[1,2,48,128]{3,2,1,0:T(8,128)} %copy.55) | copy-start | bytes 147460
  98.3 9.7 %copy-start.5 = (f32[1,2,48,128]{3,2,1,0:T(8,128)S(1)}, f32[1,2,48,128]{3,2,1,0:T(8,128)}, u32[]{:S(2)}) copy-start(f32[1,2,48,128]{3,2,1,0:T(8,128)} %copy.51) | copy-start | bytes 147460
  98.3 10.3 %copy-start.4 = (f32[1,2,48,128]{3,2,1,0:T(8,128)S(1)}, f32[1,2,48,128]{3,2,1,0:T(8,128)}, u32[]{:S(2)}) copy-start(f32[1,2,48,128]{3,2,1,0:T(8,128)} %copy.52) | copy-start | bytes 147460
  99.0 7.8 %copy-start.7 = (f32[1,2,48,128]{3,2,1,0:T(8,128)S(1)}, f32[1,2,48,128]{3,2,1,0:T(8,128)}, u32[]{:S(2)}) copy-start(f32[1,2,48,128]{3,2,1,0:T(8,128)} %copy.49) | copy-start | bytes 147460
  99.0 8.4 %copy-start.6 = (f32[1,2,48,128]{3,2,1,0:T(8,128)S(1)}, f32[1,2,48,128]{3,2,1,0:T(8,128)}, u32[]{:S(2)}) copy-start(f32[1,2,48,128]{3,2,1,0:T(8,128)} %copy.50) | copy-start | bytes 147460
  99.0 15.8 %copy-start.8 = (s32[16,2]{1,0:T(8,128)S(1)}, s32[16,2]{1,0:T(8,128)}, u32[]{:S(2)}) copy-start(s32[16,2]{1,0:T(8,128)} %get-tuple-element.2) | copy-start | bytes 388
  111.1 22.3 %all-to-all-start.2 = ((f32[16,2,48,128]{3,2,1,0:T(8,128)}), f32[16,2,48,128]{3,2,1,0:T(8,128)S(1)}, u32[]{:S(2)}, u32[]{:S(2)}) async-start(f32[16,2,48,128]{3,2,1,0:T(8,128)} %constant_dynamic-update-slice_fusion.16), calls=%async_computation.2 | async-start | bytes 1572864 | tf_op jit(solution)/shard_map/all_to_all | solution.py:19
  114.8 25.6 %copy-start.9 = (f32[768]{0:T(1024)S(1)}, f32[768]{0:T(1024)}, u32[]{:S(2)}) copy-start(f32[768]{0:T(1024)} %param.9) | copy-start | bytes 9220
  135.1 17.5 %all-to-all-start.3 = ((f32[16,48,128]{2,1,0:T(8,128)}), f32[16,48,128]{2,1,0:T(8,128)S(1)}, u32[]{:S(2)}, u32[]{:S(2)}) async-start(f32[16,48,128]{2,1,0:T(8,128)} %copy.57), calls=%async_computation.3 | async-start | bytes 786432 | tf_op jit(solution)/shard_map/all_to_all | solution.py:26
